TPU v7x, 32 devices: a whole 2x2x4 slice. The times are simulated.
32 devices in a mesh: dp: 4 (over y, core), ctx: 8 (over z, x).
Axes of the slice: x: 2, y: 2, z: 4, core: 2. Of those that a mesh axis runs over, the one named last changes fastest.
Arguments:
- queries: bfloat16 [4096, 2048], P(('dp', 'ctx')), may hold values from -6 to 6
- key_rows: bfloat16 [4096, 2048], P(('dp', 'ctx')), may hold values from -6 to 6
- value_rows: bfloat16 [4096, 2048], P(('dp', 'ctx')), may hold values from -6 to 6
- hidden_in: bfloat16 [4096, 2304], P(('dp', 'ctx')), may hold values from -6 to 6
- beta_weight: bfloat16 [2304, 16], replicated, may hold values from -0.125 to 0.125
- log_gate: float32 [16, 4096], P(None, ('dp', 'ctx')), may hold values from -1 to 0
- out_grad: bfloat16 [4096, 2048], P(('dp', 'ctx')), may hold values from -24 to 24
- lengths: int32 [4, 4], P('dp'), may hold values from 1 to 512, 1024 in all within a row
- rewards: float32 [16], replicated, may hold values from -6 to 6
- prompts: int32 [16], replicated, may hold values from 0 to 3
Outputs:
- query_grad: bfloat16 [4096, 2048], P(('dp', 'ctx'))
- key_grad: bfloat16 [4096, 2048], P(('dp', 'ctx'))
- value_grad: bfloat16 [4096, 2048], P(('dp', 'ctx'))
- gate_grad: float32 [16, 4096], P(None, ('dp', 'ctx'))
- beta_weight_grad: float32 [2304, 16], P(('dp', 'ctx'))
Inputs may be any that keep to these rules, and one draw needn't show every extreme that they name: `lengths`: each row sums to 1024; its largest entry is exactly 512.
All inputs are finite; a program needn't handle non-finite values.
Results may differ from a plain program's by a relative error of at most 0.001.
Values sent between devices are 32-bit elements; how exact they have to be, the bound alone decides.
A program may use at most 128 MiB of HBM per device.

v0:
```python
import functools

import jax
import jax.numpy as jnp
from jax import lax
from jax.experimental import pallas as pl
from jax.experimental.pallas import tpu as pltpu
from jax.sharding import PartitionSpec as P

PACK = 2
SMALL = 16
MESH = pl.DeviceIdType.MESH
F32 = jnp.float32
BF16 = jnp.bfloat16


def split(x):
    hi = x.astype(BF16)
    return hi, (x - hi.astype(F32)).astype(BF16)


def left(x):
    return jnp.concatenate(split(x), axis=1)


def left_t(x):
    return jnp.concatenate(split(x), axis=0)


def right(x):
    row = jnp.concatenate(split(x), axis=1)
    return jnp.concatenate([row, row], axis=0)


def right_t(x):
    hi, lo = split(x)
    return jnp.concatenate(
        [jnp.concatenate([hi, hi], axis=1), jnp.concatenate([lo, lo], axis=1)], axis=0
    )


def contract(a, b, dims):
    out = lax.dot_general(a, b, ((dims[:1], dims[1:]), ((), ())), preferred_element_type=F32)
    half = out.shape[1] // 2
    return out[:, :half] + out[:, half:]


def mul(a, b):
    return contract(left(a), right(b), (1, 0))


def mul_t(a, b):
    return contract(left(a), right_t(b), (1, 1))


def t_mul(a, b):
    return contract(left_t(a), right(b), (0, 0))


def stack(*parts):
    return jnp.concatenate(parts, axis=0)


def row_sum(x):
    return jnp.sum(x, axis=1, keepdims=True)


def inverses(lows, rows, cols):
    size = lows[0].shape[0]
    eye = jnp.where(rows == cols, 1.0, 0.0)
    base = min(SMALL, size)
    same = (rows // base) == (cols // base)
    powers = [jnp.where(same, -low, 0.0) for low in lows]
    totals = [eye + power for power in powers]
    powers = [mul(power, power) for power in powers]
    reach = 2
    while reach * 2 < base:
        both = [mul(stack(t, p), p) for t, p in zip(totals, powers)]
        totals = [t + b[:size] for t, b in zip(totals, both)]
        powers = [b[size:] for b in both]
        reach *= 2
    totals = [t + mul(t, p) for t, p in zip(totals, powers)]
    while base < size:
        own = ((rows // (2 * base)) == (cols // (2 * base))) & ((rows // base) != (cols // base))
        parts = [jnp.where(own, low, 0.0) for low in lows]
        mids = [mul(t, part) for t, part in zip(totals, parts)]
        totals = [t - mul(m, t) for t, m in zip(totals, mids)]
        base *= 2
    return totals


def kernel(
    q_ref, k_ref, v_ref, o_ref, cols_ref, rows_ref, hidden_ref,
    dq_ref, dk_ref, dv_ref, dgate_ref, weight_ref,
    inv_ref, mix_ref, dkk_ref, dec_ref, map_ref, fout_ref, bout_ref, fin_ref, bin_ref,
    dlogit_ref, whole_ref, near_out, near_in, far_out, far_in,
    fsend, frecv, bsend, brecv, nsend, nrecv, wsend, wrecv,
):
    tokens = q_ref.shape[0]
    groups = cols_ref.shape[0]
    width = fin_ref.shape[-1]
    count = lax.axis_size("ctx")
    seg = lax.axis_index("ctx")
    last = count - 1

    barrier = pltpu.get_barrier_semaphore()

    part = lax.axis_index("dp")
    parts = lax.axis_size("dp")
    for by in range(1, count):
        pl.semaphore_signal(
            barrier, inc=1, device_id={"ctx": lax.rem(seg + by, count)}, device_id_type=MESH
        )
    for by in range(1, parts):
        pl.semaphore_signal(
            barrier, inc=1, device_id={"dp": lax.rem(part + by, parts)}, device_id_type=MESH
        )
    pl.semaphore_wait(barrier, count + parts - 2)

    def forward_copy(group):
        return pltpu.make_async_remote_copy(
            src_ref=fout_ref.at[group], dst_ref=fin_ref.at[group],
            send_sem=fsend.at[group], recv_sem=frecv.at[group],
            device_id={"ctx": seg + 1}, device_id_type=MESH,
        )

    def backward_copy(group):
        return pltpu.make_async_remote_copy(
            src_ref=bout_ref.at[group], dst_ref=bin_ref.at[group],
            send_sem=bsend.at[group], recv_sem=brecv.at[group],
            device_id={"ctx": seg - 1}, device_id_type=MESH,
        )

    rows = lax.broadcasted_iota(jnp.int32, (tokens, tokens), 0)
    cols = lax.broadcasted_iota(jnp.int32, (tokens, tokens), 1)
    heads = range(PACK)

    def lanes(group, i):
        return pl.ds(pl.multiple_of((group * PACK + i) * width, width), width)

    def load(ref, group, i):
        return ref[:, lanes(group, i)].astype(F32)

    def token_columns(group, i):
        block = cols_ref[group]
        row_block = rows_ref[group]
        beta = block[:, i:i + 1]
        gamma = block[:, PACK + i:PACK + i + 1]
        number = block[:, 2 * PACK:2 * PACK + 1]
        weight = block[:, 2 * PACK + 1:2 * PACK + 2]
        gamma_row = row_block[i:i + 1, :]
        number_row = row_block[PACK:PACK + 1, :]
        head = jnp.where(number == 0.0, jnp.exp(gamma), 0.0)
        tied = number == number_row[:, tokens - 1:tokens]
        tail = jnp.where(
            tied, jnp.exp(jnp.where(tied, gamma_row[:, tokens - 1:tokens] - gamma, 0.0)), 0.0
        )
        return beta, gamma, number, weight, gamma_row, number_row, head, tail

    def scales(x):
        return lax.rsqrt(row_sum(x * x) + 1e-06)

    def local_part(group):
        lows, keep = [], []
        for i in heads:
            beta, gamma, number, weight, gamma_row, number_row, head, tail = token_columns(group, i)
            q, k = load(q_ref, group, i), load(k_ref, group, i)
            qh, kh = q * scales(q), k * scales(k)
            linked = (number == number_row) & (rows >= cols)
            decay = jnp.where(linked, jnp.exp(jnp.where(linked, gamma - gamma_row, 0.0)), 0.0)
            both = mul_t(stack(kh, qh), kh)
            dkk = jnp.where(rows > cols, decay * both[:tokens], 0.0)
            mix = decay * both[tokens:]
            dec_ref[group, i] = decay
            dkk_ref[group, i] = dkk
            mix_ref[group, i] = mix
            lows.append(beta * dkk)
            keep.append((beta, weight, head, tail, qh, kh, mix))
        invs = inverses(lows, rows, cols)
        for i in heads:
            inv_ref[group, i] = invs[i]
        pairs = []
        for i in heads:
            beta, weight, head, tail, qh, kh, mix = keep[i]
            v = load(v_ref, group, i)
            pairs.append(mul(invs[i], jnp.concatenate([beta * v, (beta * head) * kh], axis=1)))
        eye = jnp.where(rows == cols, 1.0, 0.0)
        for i in heads:
            beta, weight, head, tail, qh, kh, mix = keep[i]
            z = pairs[i][:, width:]
            ends = t_mul(pairs[i], tail * kh)
            fout_ref[group, i] = ends[:width]
            map_ref[group, i] = head[tokens - 1:tokens, :] * eye - ends[width:]
            carry = head * qh - mul(mix, z)
            bout_ref[group, i] = t_mul(load(o_ref, group, i) * weight, carry)

    def forward_hop(group):
        @pl.when(seg == 0)
        def _():
            fin_ref[group] = jnp.zeros_like(fin_ref[group])

        @pl.when(seg > 0)
        def _():
            forward_copy(group).wait_recv()

        @pl.when((seg > 0) & (seg < last))
        def _():
            for i in heads:
                fout_ref[group, i] = fout_ref[group, i] + mul(fin_ref[group, i], map_ref[group, i])

        @pl.when(seg < last)
        def _():
            forward_copy(group).start()

    def backward_hop(group):
        @pl.when(seg == last)
        def _():
            bin_ref[group] = jnp.zeros_like(bin_ref[group])

        @pl.when(seg < last)
        def _():
            backward_copy(group).wait_recv()

        @pl.when((seg > 0) & (seg < last))
        def _():
            for i in heads:
                bout_ref[group, i] = bout_ref[group, i] + mul_t(bin_ref[group, i], map_ref[group, i])

        @pl.when(seg > 0)
        def _():
            backward_copy(group).start()

    def gradient_part(group):
        upper = jnp.where(rows < cols, 1.0, 0.0).astype(BF16)
        upper = stack(upper, upper)
        keep = []
        for i in heads:
            beta, gamma, number, weight, gamma_row, number_row, head, tail = token_columns(group, i)
            q, k = load(q_ref, group, i), load(k_ref, group, i)
            qs, ks = scales(q), scales(k)
            qh, kh = q * qs, k * ks
            state = fin_ref[group, i]
            both = mul_t(stack(qh, kh), state)
            keep.append((beta, weight, head, tail, qs, ks, qh, kh, state, both[:tokens], both[tokens:]))
        rests = [load(v_ref, group, i) - keep[i][2] * keep[i][10] for i in heads]
        us = [mul(inv_ref[group, i], keep[i][0] * rests[i]) for i in heads]
        dos = [load(o_ref, group, i) * keep[i][1] for i in heads]
        dus = [
            t_mul(mix_ref[group, i], dos[i]) + mul_t(keep[i][3] * keep[i][7], bin_ref[group, i])
            for i in heads
        ]
        drs = [t_mul(inv_ref[group, i], dus[i]) for i in heads]
        squares = [mul_t(stack(dos[i], drs[i]), us[i]) for i in heads]
        logit_columns = []
        for i in heads:
            beta, weight, head, tail, qs, ks, qh, kh, state, qstate, kstate = keep[i]
            u, do, dr, rest, after = us[i], dos[i], drs[i], rests[i], bin_ref[group, i]
            decay, dkk = dec_ref[group, i], dkk_ref[group, i]
            dmix = squares[i][:tokens]
            dlow = jnp.where(rows > cols, -squares[i][tokens:], 0.0)
            inward = mul(stack(head * do, (-beta * head) * dr), state)
            uafter = mul(u, after)
            da = dmix * decay
            dpair = dlow * (beta * decay)
            pairs = stack(da, dpair)
            direct = mul(pairs, kh)
            turned = t_mul(pairs, stack(qh, kh))
            dqh = inward[:tokens] + direct[:tokens]
            dkh = inward[tokens:] + direct[tokens:] + turned + tail * uafter
            dq_ref[:, lanes(group, i)] = (qs * (dqh - qh * row_sum(qh * dqh))).astype(BF16)
            dk_ref[:, lanes(group, i)] = (ks * (dkh - kh * row_sum(kh * dkh))).astype(BF16)
            dv_ref[:, lanes(group, i)] = (beta * dr).astype(BF16)
            lowpart = dlow * dkk
            spread = dmix * mix_ref[group, i] + beta * lowpart
            across = lax.dot_general(
                left(spread), upper, (((1,), (0,)), ((), ())), preferred_element_type=F32
            )
            total = jnp.sum(row_sum(after * state), axis=0, keepdims=True)
            headgrad = row_sum(do * qstate) - beta * row_sum(dr * kstate)
            headgrad = head * (headgrad + jnp.where(rows[:, :1] == tokens - 1, total, 0.0))
            tailgrad = tail * row_sum(kh * uafter)
            dgate_ref[group, i:i + 1, :] = jnp.sum(
                jnp.where(rows >= cols, across + headgrad, tailgrad), axis=0, keepdims=True
            )
            dbeta = row_sum(dr * rest) + row_sum(lowpart)
            logit_columns.append(dbeta * beta * (1.0 - beta))
        dlogit_ref[group] = jnp.concatenate(logit_columns, axis=1)

    def step(t, unused):
        @pl.when(t < groups)
        def _():
            local_part(t)

        f = t - seg

        @pl.when((f >= 0) & (f < groups))
        def _():
            forward_hop(f)

        b = t - (last - seg)

        @pl.when((b >= 0) & (b < groups))
        def _():
            backward_hop(b)

        @pl.when(t >= last)
        def _():
            gradient_part(t - last)

        return unused

    lax.fori_loop(0, groups + last, step, 0)

    def drain(group, unused):
        @pl.when(seg < last)
        def _():
            forward_copy(group).wait_send()

        @pl.when(seg > 0)
        def _():
            backward_copy(group).wait_send()

        return unused

    logit_grad = jnp.concatenate([dlogit_ref[g] for g in range(groups)], axis=1)
    hidden = hidden_ref[...]
    whole_ref[...] = lax.dot_general(
        left_t(logit_grad), stack(hidden, hidden), (((0,), (0,)), ((), ())),
        preferred_element_type=F32,
    )
    owned = near_out.shape[-1]
    for p in range(parts):
        for c in range(count):
            at = (p * count + c) * owned
            near_out[p, c] = whole_ref[:, at:at + owned]

    def near_copy(by):
        to = lax.rem(part + by, parts)
        return pltpu.make_async_remote_copy(
            src_ref=near_out.at[to], dst_ref=near_in.at[by - 1],
            send_sem=nsend.at[by - 1], recv_sem=nrecv.at[by - 1],
            device_id={"dp": to}, device_id_type=MESH,
        )

    def far_copy(by):
        to = lax.rem(seg + by, count)
        return pltpu.make_async_remote_copy(
            src_ref=far_out.at[to], dst_ref=far_in.at[by - 1],
            send_sem=wsend.at[by - 1], recv_sem=wrecv.at[by - 1],
            device_id={"ctx": to}, device_id_type=MESH,
        )

    for by in range(1, parts):
        near_copy(by).start()
    total = near_out[part]
    for by in range(1, parts):
        near_copy(by).wait_recv()
        total = total + near_in[by - 1]
    far_out[...] = total
    for by in range(1, count):
        far_copy(by).start()
    total = far_out[seg]
    for by in range(1, count):
        far_copy(by).wait_recv()
        total = total + far_in[by - 1]
    weight_ref[...] = total
    for by in range(1, parts):
        near_copy(by).wait_send()
    for by in range(1, count):
        far_copy(by).wait_send()

    lax.fori_loop(0, groups, drain, 0)


def token_plan(row_lengths, positions):
    ends = jnp.cumsum(row_lengths)
    begins = ends - row_lengths
    starts = jnp.any(positions[:, None] == begins[None, :], axis=1).astype(jnp.float32)
    member = (
        (positions[:, None] >= begins[None, :]) & (positions[:, None] < ends[None, :])
    ).astype(jnp.float32)
    return (starts, member)


def advantages(rewards, prompts):
    same = (prompts[:, None] == prompts[None, :]).astype(jnp.float32)
    return rewards - jnp.sum(same * rewards[None, :], axis=1) / jnp.sum(same, axis=1)


def local(
    queries, key_rows, value_rows, hidden_in, beta_weight, log_gate, out_grad,
    lengths, rewards, prompts,
):
    tokens = queries.shape[0]
    heads = beta_weight.shape[1]
    width = queries.shape[1] // heads
    groups = heads // PACK
    ctx_count = lax.axis_size("ctx")
    roll_count = lengths.shape[1]
    group_tokens = tokens * ctx_count
    positions = lax.axis_index("ctx") * tokens + jnp.arange(tokens, dtype=jnp.int32)
    starts, member = token_plan(lengths[0], positions)
    own_advantage = lax.dynamic_slice_in_dim(
        advantages(rewards, prompts), lax.axis_index("dp") * roll_count, roll_count
    )
    roll_weight = own_advantage * group_tokens / (roll_count * lengths[0].astype(jnp.float32))
    token_weight = jnp.sum(member * roll_weight[None, :], axis=-1)
    logits = jnp.dot(hidden_in, beta_weight, preferred_element_type=jnp.float32)
    beta = jax.nn.sigmoid(logits)
    gamma = jnp.cumsum(log_gate, axis=-1)
    number = jnp.cumsum(starts)
    shared = jnp.broadcast_to(
        jnp.stack([number, token_weight], axis=1)[None], (groups, tokens, 2)
    )
    columns = jnp.concatenate(
        [
            beta.reshape(tokens, groups, PACK).transpose(1, 0, 2),
            gamma.reshape(groups, PACK, tokens).transpose(0, 2, 1),
            shared,
        ],
        axis=2,
    )
    lines = jnp.concatenate(
        [
            gamma.reshape(groups, PACK, tokens),
            jnp.broadcast_to(number[None, None], (groups, 1, tokens)),
        ],
        axis=1,
    )
    square = (groups, PACK, tokens, tokens)
    states = (groups, PACK, width, width)
    vmem = pl.BlockSpec(memory_space=pltpu.VMEM)
    model = hidden_in.shape[1]
    dp_count = lax.axis_size("dp")
    owned = model // (dp_count * ctx_count)
    dq, dk, dv, dgate, own_grad = pl.pallas_call(
        kernel,
        out_shape=(
            jax.ShapeDtypeStruct(queries.shape, BF16),
            jax.ShapeDtypeStruct(queries.shape, BF16),
            jax.ShapeDtypeStruct(queries.shape, BF16),
            jax.ShapeDtypeStruct((groups, PACK, tokens), F32),
            jax.ShapeDtypeStruct((heads, owned), F32),
        ),
        in_specs=[vmem] * 7,
        out_specs=(vmem,) * 5,
        scratch_shapes=[pltpu.VMEM(square, F32)] * 4
        + [pltpu.VMEM(states, F32)] * 5
        + [
            pltpu.VMEM((groups, tokens, PACK), F32),
            pltpu.VMEM((heads, model), F32),
            pltpu.VMEM((dp_count, ctx_count, heads, owned), F32),
            pltpu.VMEM((dp_count - 1 or 1, ctx_count, heads, owned), F32),
            pltpu.VMEM((ctx_count, heads, owned), F32),
            pltpu.VMEM((ctx_count - 1, heads, owned), F32),
        ]
        + [pltpu.SemaphoreType.DMA((groups,))] * 4
        + [pltpu.SemaphoreType.DMA((dp_count,))] * 2
        + [pltpu.SemaphoreType.DMA((ctx_count,))] * 2,
        compiler_params=pltpu.CompilerParams(
            collective_id=0, has_side_effects=True, vmem_limit_bytes=48 * 2**20
        ),
        name="delta_backward",
    )(queries, key_rows, value_rows, out_grad, columns, lines, hidden_in)
    return (dq, dk, dv, dgate.reshape(heads, tokens), own_grad.T)


def solution(mesh):
    rows = P(("dp", "ctx"), None)
    in_specs = (
        rows, rows, rows, rows, P(), P(None, ("dp", "ctx")), rows, P("dp", None), P(), P(),
    )
    out_specs = (rows, rows, rows, P(None, ("dp", "ctx")), rows)
    return jax.shard_map(local, mesh=mesh, in_specs=in_specs, out_specs=out_specs, check_vma=False)
```

profile of v0, /device:TPU:0, one launch (start us, length us, event | category | flops | bytes accessed | tf_op | source)
XLA Modules:
  0.0 103.0 jit_solution(174835280007080668)
XLA Ops:
  0.6 0.0 copy-start
  0.7 0.0 copy-start.9
  0.7 0.7 copy-done.9
  1.4 0.2 reduce-window.6
  1.5 0.1 compare_reduce_fusion
  1.6 0.0 copy-start.7
  1.6 0.0 copy-start.8
  1.6 0.6 copy-done.7
  2.3 0.0 copy-done.8
  2.3 0.2 fusion.4
  2.5 0.1 bitcast_divide_fusion
  2.6 0.1 select_reduce_fusion
  2.7 0.0 copy-done
  2.7 0.0 copy-start.6
  2.7 1.3 %fusion.2 = f32[128,16]{0,1:T(8,128)S(1)} fusion(bf16[128,2304]{1,0:T(8,128)(2,1)} %hidden_ref.1, bf16[2304,16]{0,1:T(8,128)(2,1)S(1)} %copy-done), kind=kOutput, calls=%fused_computation.3 | convolution fusion | flops 9443328 | bytes 671744 | tf_op jit(solution)/shard_map/dot_general | solution.py:408
  4.0 0.0 copy-done.6
  4.1 0.6 reduce_window_sum.28
  4.7 0.1 copy.43
  4.8 0.1 copy.42
  4.9 0.2 stack.11
  5.0 0.1 pad_maximum_fusion.1
  5.1 0.1 reduce
  5.3 0.0 copy-start.5
  5.3 0.2 copy.41
  5.6 0.0 copy-start.4
  5.6 0.2 copy.39
  5.8 0.0 copy-start.1
  5.8 0.0 copy-start.2
  5.8 0.0 copy-start.3
  5.8 0.3 pad_maximum_fusion.cols_ref
  6.2 0.2 copy-done.5
  6.4 0.3 copy-done.4
  6.6 0.3 copy-done.1
  7.0 0.2 copy-done.2
  7.1 0.2 copy-done.3
  7.3 92.1 %delta_backward.1 = (bf16[128,2048]{1,0:T(8,128)(2,1)S(1)}, bf16[128,2048]{1,0:T(8,128)(2,1)S(1)}, bf16[128,2048]{1,0:T(8,128)(2,1)S(1)}, f32[8,2,128]{2,1,0:T(2,128)S(1)}, f32[16,72]{1,0:T(8,128)S(1)}) custom-call(bf16[128,2048]{1,0:T(8,128)(2,1)S(1)} %copy-done.2, bf16[128,2048]{1,0:T(8,128)(2,1)S(1)} %copy-done.3, bf16[128,2048]{1,0:T(8,128)(2,1)S(1)} %copy-done.4, ...), custom_call_target="tpu_custom_call" | custom-call | tf_op jit(solution)/shard_map/delta_backward/pallas_call | solution.py:436
  99.4 0.8 copy.50
  100.2 0.8 copy.51
  101.0 0.8 copy.52
  101.8 0.6 copy.53
  102.4 0.6 copy.54
  (9 shorter events, 0.1 us)
Async XLA Ops:
  0.6 2.0 %copy-start = (bf16[2304,16]{0,1:T(8,128)(2,1)S(1)}, bf16[2304,16]{0,1:T(8,128)(2,1)}, u32[]{:S(2)}) copy-start(bf16[2304,16]{0,1:T(8,128)(2,1)} %param.14) | copy-start | bytes 221188
  0.7 0.7 copy-start.9
  1.6 0.7 copy-start.7
  1.6 0.7 copy-start.8
  2.7 1.4 %copy-start.6 = (f32[16,128]{1,0:T(8,128)S(1)}, f32[16,128]{1,0:T(8,128)}, u32[]{:S(2)}) copy-start(f32[16,128]{1,0:T(8,128)} %param.15) | copy-start | bytes 24580
  5.3 1.0 %copy-start.5 = (bf16[128,2048]{1,0:T(8,128)(2,1)S(1)}, bf16[128,2048]{1,0:T(8,128)(2,1)}, u32[]{:S(2)}) copy-start(bf16[128,2048]{1,0:T(8,128)(2,1)} %o_ref.1) | copy-start | bytes 1572868
  5.6 1.1 %copy-start.4 = (bf16[128,2048]{1,0:T(8,128)(2,1)S(1)}, bf16[128,2048]{1,0:T(8,128)(2,1)}, u32[]{:S(2)}) copy-start(bf16[128,2048]{1,0:T(8,128)(2,1)} %v_ref.1) | copy-start | bytes 1572868
  5.8 1.1 %copy-start.1 = (bf16[128,2304]{1,0:T(8,128)(2,1)S(1)}, bf16[128,2304]{1,0:T(8,128)(2,1)}, u32[]{:S(2)}) copy-start(bf16[128,2304]{1,0:T(8,128)(2,1)} %hidden_ref.1) | copy-start | bytes 1769476
  5.8 1.3 %copy-start.2 = (bf16[128,2048]{1,0:T(8,128)(2,1)S(1)}, bf16[128,2048]{1,0:T(8,128)(2,1)}, u32[]{:S(2)}) copy-start(bf16[128,2048]{1,0:T(8,128)(2,1)} %q_ref.1) | copy-start | bytes 1572868
  5.8 1.4 %copy-start.3 = (bf16[128,2048]{1,0:T(8,128)(2,1)S(1)}, bf16[128,2048]{1,0:T(8,128)(2,1)}, u32[]{:S(2)}) copy-start(bf16[128,2048]{1,0:T(8,128)(2,1)} %k_ref.1) | copy-start | bytes 1572868
where the time goes:
time: 103 us
  Pallas kernels  92.1 us (89%)
  local copies, waits for them, and re-layouts  6.77 us (7%)
  other arithmetic  1.93 us (2%)
  matrix products  1.33 us (1%)
    pallas_call x1, Pallas kernels, local(): pl.pallas_call(kernel, out_shape=(jax.ShapeDtypeStruct(queries.shape, BF1...  92.1 us
    unnamed x25, local copies, waits for them, and re-layouts  6.05 us

commit v1 on v0

v1 whole, which is shorter than its diff:
```python
import functools

import jax
import jax.numpy as jnp
from jax import lax
from jax.experimental import pallas as pl
from jax.experimental.pallas import tpu as pltpu
from jax.sharding import PartitionSpec as P

SMALL = 16
MAP_LAG = 2
GRAD_SLACK = 1
MESH = pl.DeviceIdType.MESH
F32 = jnp.float32
BF16 = jnp.bfloat16


def split(x):
    hi = x.astype(BF16)
    return hi, (x - hi.astype(F32)).astype(BF16)


def left(x):
    return jnp.concatenate(split(x), axis=1)


def left_t(x):
    return jnp.concatenate(split(x), axis=0)


def right(x):
    row = jnp.concatenate(split(x), axis=1)
    return jnp.concatenate([row, row], axis=0)


def right_t(x):
    hi, lo = split(x)
    return jnp.concatenate(
        [jnp.concatenate([hi, hi], axis=1), jnp.concatenate([lo, lo], axis=1)], axis=0
    )


def contract(a, b, dims):
    out = lax.dot_general(a, b, ((dims[:1], dims[1:]), ((), ())), preferred_element_type=F32)
    half = out.shape[1] // 2
    return out[:, :half] + out[:, half:]


def mul(a, b):
    return contract(left(a), right(b), (1, 0))


def mul_t(a, b):
    return contract(left(a), right_t(b), (1, 1))


def t_mul(a, b):
    return contract(left_t(a), right(b), (0, 0))


def stack(*parts):
    return jnp.concatenate(parts, axis=0)


def row_sum(x):
    return jnp.sum(x, axis=1, keepdims=True)


def inverses(lows, rows, cols):
    size = lows[0].shape[0]
    eye = jnp.where(rows == cols, 1.0, 0.0)
    base = min(SMALL, size)
    same = (rows // base) == (cols // base)
    powers = [jnp.where(same, -low, 0.0) for low in lows]
    totals = [eye + power for power in powers]
    powers = [mul(power, power) for power in powers]
    reach = 2
    while reach * 2 < base:
        both = [mul(stack(t, p), p) for t, p in zip(totals, powers)]
        totals = [t + b[:size] for t, b in zip(totals, both)]
        powers = [b[size:] for b in both]
        reach *= 2
    totals = [t + mul(t, p) for t, p in zip(totals, powers)]
    while base < size:
        own = ((rows // (2 * base)) == (cols // (2 * base))) & ((rows // base) != (cols // base))
        parts = [jnp.where(own, low, 0.0) for low in lows]
        mids = [mul(t, part) for t, part in zip(totals, parts)]
        totals = [t - mul(m, t) for t, m in zip(totals, mids)]
        base *= 2
    return totals


def kernel(
    q_ref, k_ref, v_ref, o_ref, cols_ref, rows_ref, hidden_ref,
    dq_ref, dk_ref, dv_ref, dgate_ref, weight_ref,
    inv_ref, mix_ref, dkk_ref, dec_ref, maps_ref, give_ref,
    fpair_ref, bpair_ref, fout_ref, bout_ref, fmate_ref, bmate_ref,
    dlogit_ref, whole_ref, near_out, near_in, far_out, far_in,
    msend, mrecv, fsend, frecv, bsend, brecv, fgive, ftake, bgive, btake,
    nsend, nrecv, wsend, wrecv,
):
    tokens = q_ref.shape[0]
    width = fout_ref.shape[-1]
    turns = fout_ref.shape[0]
    count = lax.axis_size("ctx")
    seg = lax.axis_index("ctx")
    tiers = count // 2
    tier = seg // 2
    side = lax.rem(seg, 2)
    mate = seg + 1 - 2 * side

    barrier = pltpu.get_barrier_semaphore()

    part = lax.axis_index("dp")
    parts = lax.axis_size("dp")
    for by in range(1, count):
        pl.semaphore_signal(
            barrier, inc=1, device_id={"ctx": lax.rem(seg + by, count)}, device_id_type=MESH
        )
    for by in range(1, parts):
        pl.semaphore_signal(
            barrier, inc=1, device_id={"dp": lax.rem(part + by, parts)}, device_id_type=MESH
        )
    pl.semaphore_wait(barrier, count + parts - 2)

    def copy(src, dst, sent, landed, to):
        return pltpu.make_async_remote_copy(
            src_ref=src, dst_ref=dst, send_sem=sent, recv_sem=landed,
            device_id={"ctx": to}, device_id_type=MESH,
        )

    def map_copy(i):
        return copy(give_ref.at[i], maps_ref.at[i, side], msend.at[i], mrecv.at[i], mate)

    def forward_copy(i):
        return copy(fout_ref.at[i], fpair_ref.at[i, 0], fsend.at[i], frecv.at[i], seg + 2)

    def backward_copy(i):
        return copy(bout_ref.at[i], bpair_ref.at[i, 1], bsend.at[i], brecv.at[i], seg - 2)

    def state_copy(i):
        return copy(fpair_ref.at[i, 1 - side], fmate_ref.at[i], fgive.at[i], ftake.at[i], mate)

    def after_copy(i):
        return copy(bpair_ref.at[i, 1 - side], bmate_ref.at[i], bgive.at[i], btake.at[i], mate)

    rows = lax.broadcasted_iota(jnp.int32, (tokens, tokens), 0)
    cols = lax.broadcasted_iota(jnp.int32, (tokens, tokens), 1)
    both_heads = range(2)

    def head_of(turn, j):
        return (side if j == 0 else 1 - side) * turns + turn

    def lanes(h):
        return pl.ds(pl.multiple_of(h * width, width), width)

    def load(ref, h):
        return ref[:, lanes(h)].astype(F32)

    def token_columns(h):
        block = cols_ref[h]
        row_block = rows_ref[h]
        beta, gamma = block[:, 0:1], block[:, 1:2]
        number, weight = block[:, 2:3], block[:, 3:4]
        gamma_row, number_row = row_block[0:1, :], row_block[1:2, :]
        head = jnp.where(number == 0.0, jnp.exp(gamma), 0.0)
        tied = number == number_row[:, tokens - 1:tokens]
        tail = jnp.where(
            tied, jnp.exp(jnp.where(tied, gamma_row[:, tokens - 1:tokens] - gamma, 0.0)), 0.0
        )
        return beta, gamma, number, weight, gamma_row, number_row, head, tail

    def scales(x):
        return lax.rsqrt(row_sum(x * x) + 1e-06)

    def local_part(turn):
        lows, keep = [], []
        for j in both_heads:
            h = head_of(turn, j)
            beta, gamma, number, weight, gamma_row, number_row, head, tail = token_columns(h)
            q, k = load(q_ref, h), load(k_ref, h)
            qh, kh = q * scales(q), k * scales(k)
            linked = (number == number_row) & (rows >= cols)
            decay = jnp.where(linked, jnp.exp(jnp.where(linked, gamma - gamma_row, 0.0)), 0.0)
            both = mul_t(stack(kh, qh), kh)
            dkk = jnp.where(rows > cols, decay * both[:tokens], 0.0)
            mix = decay * both[tokens:]
            dec_ref[turn, j] = decay
            dkk_ref[turn, j] = dkk
            mix_ref[turn, j] = mix
            lows.append(beta * dkk)
            keep.append((h, beta, weight, head, tail, qh, kh, mix))
        invs = inverses(lows, rows, cols)
        for j in both_heads:
            inv_ref[turn, j] = invs[j]
        pairs = []
        for j in both_heads:
            h, beta, weight, head, tail, qh, kh, mix = keep[j]
            v = load(v_ref, h)
            pairs.append(mul(invs[j], jnp.concatenate([beta * v, (beta * head) * kh], axis=1)))
        eye = jnp.where(rows == cols, 1.0, 0.0)
        for j in both_heads:
            h, beta, weight, head, tail, qh, kh, mix = keep[j]
            out = maps_ref.at[turn, side] if j == 0 else give_ref.at[turn]
            z = pairs[j][:, width:]
            ends = t_mul(pairs[j], tail * kh)
            out[0] = head[tokens - 1:tokens, :] * eye - ends[width:]
            out[1] = ends[:width]
            carry = head * qh - mul(mix, z)
            out[2] = t_mul(load(o_ref, h) * weight, carry)

    def forward_step(i):
        @pl.when(tier == 0)
        def _():
            fpair_ref[i, 0] = jnp.zeros((width, width), F32)

        @pl.when(tier > 0)
        def _():
            forward_copy(i).wait_recv()

        second = mul(fpair_ref[i, 0], maps_ref[i, 0, 0]) + maps_ref[i, 0, 1]
        fpair_ref[i, 1] = second

        @pl.when(tier < tiers - 1)
        def _():
            fout_ref[i] = mul(fpair_ref[i, 1], maps_ref[i, 1, 0]) + maps_ref[i, 1, 1]
            forward_copy(i).start()

        state_copy(i).start()

    def backward_step(i):
        @pl.when(tier == tiers - 1)
        def _():
            bpair_ref[i, 1] = jnp.zeros((width, width), F32)

        @pl.when(tier < tiers - 1)
        def _():
            backward_copy(i).wait_recv()

        first = mul_t(bpair_ref[i, 1], maps_ref[i, 1, 0]) + maps_ref[i, 1, 2]
        bpair_ref[i, 0] = first

        @pl.when(tier > 0)
        def _():
            bout_ref[i] = mul_t(bpair_ref[i, 0], maps_ref[i, 0, 0]) + maps_ref[i, 0, 2]
            backward_copy(i).start()

        after_copy(i).start()

    def gradient_part(turn):
        state_copy(turn).wait_recv()
        after_copy(turn).wait_recv()
        upper = jnp.where(rows < cols, 1.0, 0.0).astype(BF16)
        upper = stack(upper, upper)
        keep = []
        afters = [bpair_ref[turn, side], bmate_ref[turn]]
        for j in both_heads:
            h = head_of(turn, j)
            beta, gamma, number, weight, gamma_row, number_row, head, tail = token_columns(h)
            q, k = load(q_ref, h), load(k_ref, h)
            qs, ks = scales(q), scales(k)
            qh, kh = q * qs, k * ks
            state = fpair_ref[turn, side] if j == 0 else fmate_ref[turn]
            both = mul_t(stack(qh, kh), state)
            keep.append((beta, weight, head, tail, qs, ks, qh, kh, state, both[:tokens], both[tokens:]))
        heads = [head_of(turn, j) for j in both_heads]
        rests = [load(v_ref, heads[i]) - keep[i][2] * keep[i][10] for i in both_heads]
        us = [mul(inv_ref[turn, i], keep[i][0] * rests[i]) for i in both_heads]
        dos = [load(o_ref, heads[i]) * keep[i][1] for i in both_heads]
        dus = [
            t_mul(mix_ref[turn, i], dos[i]) + mul_t(keep[i][3] * keep[i][7], afters[i])
            for i in both_heads
        ]
        drs = [t_mul(inv_ref[turn, i], dus[i]) for i in both_heads]
        squares = [mul_t(stack(dos[i], drs[i]), us[i]) for i in both_heads]
        for i in both_heads:
            beta, weight, head, tail, qs, ks, qh, kh, state, qstate, kstate = keep[i]
            h = heads[i]
            u, do, dr, rest, after = us[i], dos[i], drs[i], rests[i], afters[i]
            decay, dkk = dec_ref[turn, i], dkk_ref[turn, i]
            dmix = squares[i][:tokens]
            dlow = jnp.where(rows > cols, -squares[i][tokens:], 0.0)
            inward = mul(stack(head * do, (-beta * head) * dr), state)
            uafter = mul(u, after)
            da = dmix * decay
            dpair = dlow * (beta * decay)
            pairs = stack(da, dpair)
            direct = mul(pairs, kh)
            turned = t_mul(pairs, stack(qh, kh))
            dqh = inward[:tokens] + direct[:tokens]
            dkh = inward[tokens:] + direct[tokens:] + turned + tail * uafter
            dq_ref[:, lanes(h)] = (qs * (dqh - qh * row_sum(qh * dqh))).astype(BF16)
            dk_ref[:, lanes(h)] = (ks * (dkh - kh * row_sum(kh * dkh))).astype(BF16)
            dv_ref[:, lanes(h)] = (beta * dr).astype(BF16)
            lowpart = dlow * dkk
            spread = dmix * mix_ref[turn, i] + beta * lowpart
            across = lax.dot_general(
                left(spread), upper, (((1,), (0,)), ((), ())), preferred_element_type=F32
            )
            total = jnp.sum(row_sum(after * state), axis=0, keepdims=True)
            headgrad = row_sum(do * qstate) - beta * row_sum(dr * kstate)
            headgrad = head * (headgrad + jnp.where(rows[:, :1] == tokens - 1, total, 0.0))
            tailgrad = tail * row_sum(kh * uafter)
            dgate_ref[h] = jnp.sum(
                jnp.where(rows >= cols, across + headgrad, tailgrad), axis=0, keepdims=True
            )
            dbeta = row_sum(dr * rest) + row_sum(lowpart)
            dlogit_ref[h] = dbeta * beta * (1.0 - beta)

    def within(i):
        return (i >= 0) & (i < turns)

    grad_lag = MAP_LAG + tiers + GRAD_SLACK

    def step(t, unused):
        @pl.when(t < turns)
        def _():
            local_part(t)
            map_copy(t).start()

        f = t - MAP_LAG - tier
        b = t - MAP_LAG - (tiers - 1 - tier)
        m = jnp.maximum(f, b)

        @pl.when(within(m))
        def _():
            map_copy(m).wait_recv()

        @pl.when(within(f))
        def _():
            forward_step(f)

        @pl.when(within(b))
        def _():
            backward_step(b)

        @pl.when(within(t - grad_lag))
        def _():
            gradient_part(t - grad_lag)

        return unused

    lax.fori_loop(0, turns + grad_lag, step, 0)

    def drain(i, unused):
        map_copy(i).wait_send()
        state_copy(i).wait_send()
        after_copy(i).wait_send()

        @pl.when(tier < tiers - 1)
        def _():
            forward_copy(i).wait_send()

        @pl.when(tier > 0)
        def _():
            backward_copy(i).wait_send()

        return unused

    logit_grad = jnp.concatenate([dlogit_ref[h] for h in range(2 * turns)], axis=1)
    hidden = hidden_ref[...]
    whole_ref[...] = lax.dot_general(
        left_t(logit_grad), stack(hidden, hidden), (((0,), (0,)), ((), ())),
        preferred_element_type=F32,
    )
    owned = near_out.shape[-1]
    for p in range(parts):
        for c in range(count):
            at = (p * count + c) * owned
            near_out[p, c] = whole_ref[:, at:at + owned]

    def near_copy(by):
        to = lax.rem(part + by, parts)
        return pltpu.make_async_remote_copy(
            src_ref=near_out.at[to], dst_ref=near_in.at[by - 1],
            send_sem=nsend.at[by - 1], recv_sem=nrecv.at[by - 1],
            device_id={"dp": to}, device_id_type=MESH,
        )

    def far_copy(by):
        to = lax.rem(seg + by, count)
        return pltpu.make_async_remote_copy(
            src_ref=far_out.at[to], dst_ref=far_in.at[by - 1],
            send_sem=wsend.at[by - 1], recv_sem=wrecv.at[by - 1],
            device_id={"ctx": to}, device_id_type=MESH,
        )

    for by in range(1, parts):
        near_copy(by).start()
    total = near_out[part]
    for by in range(1, parts):
        near_copy(by).wait_recv()
        total = total + near_in[by - 1]
    far_out[...] = total
    for by in range(1, count):
        far_copy(by).start()
    total = far_out[seg]
    for by in range(1, count):
        far_copy(by).wait_recv()
        total = total + far_in[by - 1]
    weight_ref[...] = total
    for by in range(1, parts):
        near_copy(by).wait_send()
    for by in range(1, count):
        far_copy(by).wait_send()

    lax.fori_loop(0, turns, drain, 0)


def token_plan(row_lengths, positions):
    ends = jnp.cumsum(row_lengths)
    begins = ends - row_lengths
    starts = jnp.any(positions[:, None] == begins[None, :], axis=1).astype(jnp.float32)
    member = (
        (positions[:, None] >= begins[None, :]) & (positions[:, None] < ends[None, :])
    ).astype(jnp.float32)
    return (starts, member)


def advantages(rewards, prompts):
    same = (prompts[:, None] == prompts[None, :]).astype(jnp.float32)
    return rewards - jnp.sum(same * rewards[None, :], axis=1) / jnp.sum(same, axis=1)


def local(
    queries, key_rows, value_rows, hidden_in, beta_weight, log_gate, out_grad,
    lengths, rewards, prompts,
):
    tokens = queries.shape[0]
    heads = beta_weight.shape[1]
    width = queries.shape[1] // heads
    ctx_count = lax.axis_size("ctx")
    roll_count = lengths.shape[1]
    group_tokens = tokens * ctx_count
    positions = lax.axis_index("ctx") * tokens + jnp.arange(tokens, dtype=jnp.int32)
    starts, member = token_plan(lengths[0], positions)
    own_advantage = lax.dynamic_slice_in_dim(
        advantages(rewards, prompts), lax.axis_index("dp") * roll_count, roll_count
    )
    roll_weight = own_advantage * group_tokens / (roll_count * lengths[0].astype(jnp.float32))
    token_weight = jnp.sum(member * roll_weight[None, :], axis=-1)
    logits = jnp.dot(hidden_in, beta_weight, preferred_element_type=jnp.float32)
    beta = jax.nn.sigmoid(logits)
    gamma = jnp.cumsum(log_gate, axis=-1)
    number = jnp.cumsum(starts)
    shared = jnp.broadcast_to(
        jnp.stack([number, token_weight], axis=1)[None], (heads, tokens, 2)
    )
    columns = jnp.concatenate([beta.T[:, :, None], gamma[:, :, None], shared], axis=2)
    lines = jnp.stack([gamma, jnp.broadcast_to(number[None], (heads, tokens))], axis=1)
    turns = heads // 2
    square = (turns, 2, tokens, tokens)
    states = (turns, width, width)
    pairs = (turns, 2, width, width)
    vmem = pl.BlockSpec(memory_space=pltpu.VMEM)
    model = hidden_in.shape[1]
    dp_count = lax.axis_size("dp")
    owned = model // (dp_count * ctx_count)
    dq, dk, dv, dgate, own_grad = pl.pallas_call(
        kernel,
        out_shape=(
            jax.ShapeDtypeStruct(queries.shape, BF16),
            jax.ShapeDtypeStruct(queries.shape, BF16),
            jax.ShapeDtypeStruct(queries.shape, BF16),
            jax.ShapeDtypeStruct((heads, 1, tokens), F32),
            jax.ShapeDtypeStruct((heads, owned), F32),
        ),
        in_specs=[vmem] * 7,
        out_specs=(vmem,) * 5,
        scratch_shapes=[pltpu.VMEM(square, F32)] * 4
        + [
            pltpu.VMEM((turns, 2, 3, width, width), F32),
            pltpu.VMEM((turns, 3, width, width), F32),
        ]
        + [pltpu.VMEM(pairs, F32)] * 2
        + [pltpu.VMEM(states, F32)] * 4
        + [
            pltpu.VMEM((heads, tokens, 1), F32),
            pltpu.VMEM((heads, model), F32),
            pltpu.VMEM((dp_count, ctx_count, heads, owned), F32),
            pltpu.VMEM((dp_count - 1 or 1, ctx_count, heads, owned), F32),
            pltpu.VMEM((ctx_count, heads, owned), F32),
            pltpu.VMEM((ctx_count - 1, heads, owned), F32),
        ]
        + [pltpu.SemaphoreType.DMA((turns,))] * 10
        + [pltpu.SemaphoreType.DMA((dp_count,))] * 2
        + [pltpu.SemaphoreType.DMA((ctx_count,))] * 2,
        compiler_params=pltpu.CompilerParams(
            collective_id=0, has_side_effects=True, vmem_limit_bytes=48 * 2**20
        ),
        name="delta_backward",
    )(queries, key_rows, value_rows, out_grad, columns, lines, hidden_in)
    return (dq, dk, dv, dgate.reshape(heads, tokens), own_grad.T)


def solution(mesh):
    rows = P(("dp", "ctx"), None)
    in_specs = (
        rows, rows, rows, rows, P(), P(None, ("dp", "ctx")), rows, P("dp", None), P(), P(),
    )
    out_specs = (rows, rows, rows, P(None, ("dp", "ctx")), rows)
    return jax.shard_map(local, mesh=mesh, in_specs=in_specs, out_specs=out_specs, check_vma=False)
```

time: 103 us -> 92.1 us (0.89)
  Pallas kernels: 92.1 us -> 81.1 us
    pallas_call x1, Pallas kernels: 92.1 us -> 81.1 us  [local(): pl.pallas_call(kernel, out_shape=(jax.ShapeDtypeStruct(queries.shape, BF1...]
where the time goes in v1:
time: 92.1 us; the launch traced here: 91.8 us
  Pallas kernels  81.1 us (88%)
  local copies, waits for them, and re-layouts  7.27 us (8%)
  matrix products  1.41 us (2%)
  other arithmetic  1.24 us (1%)
    pallas_call x1, Pallas kernels, local(): pl.pallas_call(kernel, out_shape=(jax.ShapeDtypeStruct(queries.shape, BF1...  81.1 us
    unnamed x25, local copies, waits for them, and re-layouts  6.7 us

profile of v1, /device:TPU:0, one launch (start us, length us, event | category | flops | bytes accessed | tf_op | source)
XLA Modules:
  0.0 91.8 jit_solution(9024234724786772932)
XLA Ops:
  0.6 0.0 copy-start
  0.7 0.0 copy-start.9
  0.7 0.7 copy-done.9
  1.4 0.2 reduce-window.6
  1.5 0.0 copy-start.7
  1.5 0.0 copy-start.8
  1.5 0.1 compare_reduce_fusion
  1.6 0.0 copy-start.6
  1.6 0.6 copy-done.7
  2.2 0.0 copy-done.8
  2.2 0.2 fusion.5
  2.4 0.1 bitcast_divide_fusion
  2.5 0.1 select_reduce_fusion
  2.6 0.0 copy-done.6
  2.6 0.3 reduce_window_sum.25
  2.9 0.0 copy-done
  2.9 0.0 copy-start.3
  2.9 0.0 copy-start.4
  2.9 1.4 %fusion.3 = f32[16,128,1]{1,0,2:T(8,128)S(1)} fusion(bf16[2304,16]{0,1:T(8,128)(2,1)S(1)} %copy-done, bf16[128,2304]{1,0:T(8,128)(2,1)} %hidden_ref.1), kind=kOutput, calls=%fused_computation.4 | convolution fusion | flops 9443328 | bytes 671744 | tf_op jit(solution)/shard_map/dot_general | solution.py:442
  4.3 0.1 copy.24
  4.4 0.2 stack.17
  4.6 0.1 reduce
  4.7 0.1 copy.25
  4.8 0.0 copy-start.1
  4.9 0.0 copy-start.2
  4.9 0.4 copy.26.cols_ref
  5.3 0.0 copy-done.3
  5.3 0.0 copy-done.4
  5.3 0.6 copy-done.1
  5.9 0.2 copy-done.2
  6.1 0.0 copy-start.5
  6.1 1.0 %copy-done.5 = bf16[128,2048]{1,0:T(8,128)(2,1)S(1)} copy-done((bf16[128,2048]{1,0:T(8,128)(2,1)S(1)}, bf16[128,2048]{1,0:T(8,128)(2,1)}, u32[]{:S(2)}) %copy-start.5) | copy-done | bytes 524312
  7.1 81.1 %delta_backward.1 = (bf16[128,2048]{1,0:T(8,128)(2,1)S(1)}, bf16[128,2048]{1,0:T(8,128)(2,1)S(1)}, bf16[128,2048]{1,0:T(8,128)(2,1)S(1)}, f32[16,1,128]{2,1,0:T(1,128)S(1)}, f32[16,72]{1,0:T(8,128)S(1)}) custom-call(bf16[128,2048]{1,0:T(8,128)(2,1)S(1)} %copy-done.2, bf16[128,2048]{1,0:T(8,128)(2,1)S(1)} %copy-done.3, bf16[128,2048]{1,0:T(8,128)(2,1)S(1)} %copy-done.4, ...), custom_call_target="tpu_custom_call" | custom-call | tf_op jit(solution)/shard_map/delta_backward/pallas_call | solution.py:459
  88.2 0.8 copy.32
  89.0 0.8 copy.33
  89.8 0.8 copy.34
  90.6 0.6 copy.35
  91.2 0.6 copy.36
  (9 shorter events, 0.1 us)
Async XLA Ops:
  0.6 2.2 %copy-start = (bf16[2304,16]{0,1:T(8,128)(2,1)S(1)}, bf16[2304,16]{0,1:T(8,128)(2,1)}, u32[]{:S(2)}) copy-start(bf16[2304,16]{0,1:T(8,128)(2,1)} %param.14) | copy-start | bytes 221188
  0.7 0.7 copy-start.9
  1.5 0.7 copy-start.7
  1.5 0.7 copy-start.8
  1.6 0.9 %copy-start.6 = (f32[16,128]{1,0:T(8,128)S(1)}, f32[16,128]{1,0:T(8,128)}, u32[]{:S(2)}) copy-start(f32[16,128]{1,0:T(8,128)} %param.15) | copy-start | bytes 24580
  2.9 2.4 %copy-start.3 = (bf16[128,2048]{1,0:T(8,128)(2,1)S(1)}, bf16[128,2048]{1,0:T(8,128)(2,1)}, u32[]{:S(2)}) copy-start(bf16[128,2048]{1,0:T(8,128)(2,1)} %k_ref.1) | copy-start | bytes 1572868
  2.9 2.4 %copy-start.4 = (bf16[128,2048]{1,0:T(8,128)(2,1)S(1)}, bf16[128,2048]{1,0:T(8,128)(2,1)}, u32[]{:S(2)}) copy-start(bf16[128,2048]{1,0:T(8,128)(2,1)} %v_ref.1) | copy-start | bytes 1572868
  4.8 1.1 %copy-start.1 = (bf16[128,2304]{1,0:T(8,128)(2,1)S(1)}, bf16[128,2304]{1,0:T(8,128)(2,1)}, u32[]{:S(2)}) copy-start(bf16[128,2304]{1,0:T(8,128)(2,1)} %hidden_ref.1) | copy-start | bytes 1769476
  4.9 1.2 %copy-start.2 = (bf16[128,2048]{1,0:T(8,128)(2,1)S(1)}, bf16[128,2048]{1,0:T(8,128)(2,1)}, u32[]{:S(2)}) copy-start(bf16[128,2048]{1,0:T(8,128)(2,1)} %q_ref.1) | copy-start | bytes 1572868
  6.1 1.0 %copy-start.5 = (bf16[128,2048]{1,0:T(8,128)(2,1)S(1)}, bf16[128,2048]{1,0:T(8,128)(2,1)}, u32[]{:S(2)}) copy-start(bf16[128,2048]{1,0:T(8,128)(2,1)} %o_ref.1) | copy-start | bytes 1572868

commit v2 on v1

--- a/solution.py
+++ b/solution.py
@@ -91,8 +91,11 @@
 
 
 def kernel(
-    q_ref, k_ref, v_ref, o_ref, cols_ref, rows_ref, hidden_ref,
+    length_in, reward_in, prompt_in,
+    q_in, k_in, v_in, o_in, hidden_in, proj_in, gate_in,
     dq_ref, dk_ref, dv_ref, dgate_ref, weight_ref,
+    length_ref, reward_ref, prompt_ref,
+    q_ref, k_ref, v_ref, o_ref, hidden_ref, proj_ref, gate_ref, cols_ref, rows_ref, load_sem,
     inv_ref, mix_ref, dkk_ref, dec_ref, maps_ref, give_ref,
     fpair_ref, bpair_ref, fout_ref, bout_ref, fmate_ref, bmate_ref,
     dlogit_ref, whole_ref, near_out, near_in, far_out, far_in,
@@ -109,6 +112,17 @@
     side = lax.rem(seg, 2)
     mate = seg + 1 - 2 * side
 
+    loads = [
+        pltpu.make_async_copy(src, dst, load_sem.at[n])
+        for n, (src, dst) in enumerate([
+            (length_in, length_ref), (reward_in, reward_ref), (prompt_in, prompt_ref),
+            (gate_in, gate_ref), (proj_in, proj_ref), (hidden_in, hidden_ref), (k_in, k_ref),
+            (q_in, q_ref), (v_in, v_ref), (o_in, o_ref),
+        ])
+    ]
+    for load_copy in loads:
+        load_copy.start()
+
     barrier = pltpu.get_barrier_semaphore()
 
     part = lax.axis_index("dp")
@@ -121,6 +135,67 @@
         pl.semaphore_signal(
             barrier, inc=1, device_id={"dp": lax.rem(part + by, parts)}, device_id_type=MESH
         )
+
+    rows = lax.broadcasted_iota(jnp.int32, (tokens, tokens), 0)
+    cols = lax.broadcasted_iota(jnp.int32, (tokens, tokens), 1)
+
+    for load_copy in loads[:3]:
+        load_copy.wait()
+    rolls = length_ref.shape[1]
+    amounts = []
+    for i in range(rolls):
+        own = prompt_ref[part * rolls + i]
+        total, members = jnp.zeros((1, tokens), F32), jnp.zeros((1, tokens), F32)
+        for j in range(reward_ref.shape[0]):
+            same = jnp.where(prompt_ref[j] == own, 1.0, 0.0)
+            total = total + same * reward_ref[j]
+            members = members + same
+        advantage = reward_ref[part * rolls + i] - total / members
+        length = jnp.zeros((1, tokens), F32) + length_ref[0, i].astype(F32)
+        amounts.append(advantage * (tokens * count) / (rolls * length))
+
+    def plan(spots, spread_out):
+        number, weight = jnp.zeros(spots.shape, F32), jnp.zeros(spots.shape, F32)
+        begin = 0
+        for i in range(rolls):
+            end = begin + length_ref[0, i]
+            started = (spots >= begin) & (begin >= seg * tokens)
+            number = number + jnp.where(started, 1.0, 0.0)
+            amount = spread_out(amounts[i])
+            weight = weight + jnp.where((spots >= begin) & (spots < end), amount, 0.0)
+            begin = end
+        return number, weight
+
+    number_row, _ = plan(seg * tokens + cols[:1, :], lambda x: x)
+    number_col, weight_col = plan(seg * tokens + rows[:, :1], lambda x: x[:, :1])
+
+    def thirds(x):
+        first = x.astype(BF16)
+        rest = x - first.astype(F32)
+        second = rest.astype(BF16)
+        return first, second, (rest - second.astype(F32)).astype(BF16)
+
+    loads[3].wait()
+    upto = jnp.where(rows <= cols, 1.0, 0.0).astype(BF16)
+    gates = jnp.concatenate(thirds(gate_ref[...]), axis=0)
+    heads_all = gate_ref.shape[0]
+    sums = lax.dot_general(gates, upto, (((1,), (0,)), ((), ())), preferred_element_type=F32)
+    gamma_rows = (sums[2 * heads_all:] + sums[heads_all:2 * heads_all]) + sums[:heads_all]
+    for h in range(heads_all):
+        rows_ref[h] = jnp.concatenate([gamma_rows[h:h + 1], number_row], axis=0)
+    gamma_cols = gamma_rows.T
+    loads[4].wait()
+    loads[5].wait()
+    logits = lax.dot_general(
+        hidden_ref[...], proj_ref[...], (((1,), (1,)), ((), ())), preferred_element_type=F32
+    )
+    betas = jax.nn.sigmoid(logits)
+    for h in range(heads_all):
+        cols_ref[h] = jnp.concatenate(
+            [betas[:, h:h + 1], gamma_cols[:, h:h + 1], number_col, weight_col], axis=1
+        )
+    for load_copy in loads[6:]:
+        load_copy.wait()
     pl.semaphore_wait(barrier, count + parts - 2)
 
     def copy(src, dst, sent, landed, to):
@@ -144,8 +219,6 @@
     def after_copy(i):
         return copy(bpair_ref.at[i, 1 - side], bmate_ref.at[i], bgive.at[i], btake.at[i], mate)
 
-    rows = lax.broadcasted_iota(jnp.int32, (tokens, tokens), 0)
-    cols = lax.broadcasted_iota(jnp.int32, (tokens, tokens), 1)
     both_heads = range(2)
 
     def head_of(turn, j):
@@ -301,7 +374,7 @@
             headgrad = row_sum(do * qstate) - beta * row_sum(dr * kstate)
             headgrad = head * (headgrad + jnp.where(rows[:, :1] == tokens - 1, total, 0.0))
             tailgrad = tail * row_sum(kh * uafter)
-            dgate_ref[h] = jnp.sum(
+            dgate_ref[pl.ds(h, 1), :] = jnp.sum(
                 jnp.where(rows >= cols, across + headgrad, tailgrad), axis=0, keepdims=True
             )
             dbeta = row_sum(dr * rest) + row_sum(lowpart)
@@ -407,19 +480,14 @@
     lax.fori_loop(0, turns, drain, 0)
 
 
-def token_plan(row_lengths, positions):
-    ends = jnp.cumsum(row_lengths)
-    begins = ends - row_lengths
-    starts = jnp.any(positions[:, None] == begins[None, :], axis=1).astype(jnp.float32)
-    member = (
-        (positions[:, None] >= begins[None, :]) & (positions[:, None] < ends[None, :])
-    ).astype(jnp.float32)
-    return (starts, member)
-
-
-def advantages(rewards, prompts):
-    same = (prompts[:, None] == prompts[None, :]).astype(jnp.float32)
-    return rewards - jnp.sum(same * rewards[None, :], axis=1) / jnp.sum(same, axis=1)
+def move_kernel(*refs):
+    half = len(refs) // 2
+    sems = refs[-1]
+    copies = [pltpu.make_async_copy(refs[n], refs[half + n], sems.at[n]) for n in range(half)]
+    for move in copies:
+        move.start()
+    for move in copies:
+        move.wait()
 
 
 def local(
@@ -430,44 +498,42 @@
     heads = beta_weight.shape[1]
     width = queries.shape[1] // heads
     ctx_count = lax.axis_size("ctx")
-    roll_count = lengths.shape[1]
-    group_tokens = tokens * ctx_count
-    positions = lax.axis_index("ctx") * tokens + jnp.arange(tokens, dtype=jnp.int32)
-    starts, member = token_plan(lengths[0], positions)
-    own_advantage = lax.dynamic_slice_in_dim(
-        advantages(rewards, prompts), lax.axis_index("dp") * roll_count, roll_count
-    )
-    roll_weight = own_advantage * group_tokens / (roll_count * lengths[0].astype(jnp.float32))
-    token_weight = jnp.sum(member * roll_weight[None, :], axis=-1)
-    logits = jnp.dot(hidden_in, beta_weight, preferred_element_type=jnp.float32)
-    beta = jax.nn.sigmoid(logits)
-    gamma = jnp.cumsum(log_gate, axis=-1)
-    number = jnp.cumsum(starts)
-    shared = jnp.broadcast_to(
-        jnp.stack([number, token_weight], axis=1)[None], (heads, tokens, 2)
-    )
-    columns = jnp.concatenate([beta.T[:, :, None], gamma[:, :, None], shared], axis=2)
-    lines = jnp.stack([gamma, jnp.broadcast_to(number[None], (heads, tokens))], axis=1)
     turns = heads // 2
     square = (turns, 2, tokens, tokens)
     states = (turns, width, width)
     pairs = (turns, 2, width, width)
     vmem = pl.BlockSpec(memory_space=pltpu.VMEM)
+    hbm = pl.BlockSpec(memory_space=pltpu.HBM)
     model = hidden_in.shape[1]
     dp_count = lax.axis_size("dp")
     owned = model // (dp_count * ctx_count)
-    dq, dk, dv, dgate, own_grad = pl.pallas_call(
+    out_shape = (
+        jax.ShapeDtypeStruct(queries.shape, BF16),
+        jax.ShapeDtypeStruct(queries.shape, BF16),
+        jax.ShapeDtypeStruct(queries.shape, BF16),
+        jax.ShapeDtypeStruct((heads, tokens), F32),
+        jax.ShapeDtypeStruct((heads, owned), F32),
+    )
+    grads = pl.pallas_call(
         kernel,
-        out_shape=(
-            jax.ShapeDtypeStruct(queries.shape, BF16),
-            jax.ShapeDtypeStruct(queries.shape, BF16),
-            jax.ShapeDtypeStruct(queries.shape, BF16),
-            jax.ShapeDtypeStruct((heads, 1, tokens), F32),
-            jax.ShapeDtypeStruct((heads, owned), F32),
-        ),
-        in_specs=[vmem] * 7,
+        out_shape=out_shape,
+        in_specs=[hbm] * 10,
         out_specs=(vmem,) * 5,
-        scratch_shapes=[pltpu.VMEM(square, F32)] * 4
+        scratch_shapes=[
+            pltpu.SMEM(lengths.shape, jnp.int32),
+            pltpu.SMEM(rewards.shape, F32),
+            pltpu.SMEM(prompts.shape, jnp.int32),
+        ]
+        + [pltpu.VMEM(queries.shape, BF16)] * 4
+        + [
+            pltpu.VMEM(hidden_in.shape, BF16),
+            pltpu.VMEM((heads, model), BF16),
+            pltpu.VMEM(log_gate.shape, F32),
+            pltpu.VMEM((heads, tokens, 4), F32),
+            pltpu.VMEM((heads, 2, tokens), F32),
+            pltpu.SemaphoreType.DMA((10,)),
+        ]
+        + [pltpu.VMEM(square, F32)] * 4
         + [
             pltpu.VMEM((turns, 2, 3, width, width), F32),
             pltpu.VMEM((turns, 3, width, width), F32),
@@ -489,8 +555,22 @@
             collective_id=0, has_side_effects=True, vmem_limit_bytes=48 * 2**20
         ),
         name="delta_backward",
-    )(queries, key_rows, value_rows, out_grad, columns, lines, hidden_in)
-    return (dq, dk, dv, dgate.reshape(heads, tokens), own_grad.T)
+    )(
+        *[pltpu.with_memory_space_constraint(x, pltpu.HBM) for x in (
+            lengths, rewards, prompts,
+            queries, key_rows, value_rows, out_grad, hidden_in, beta_weight.T, log_gate,
+        )],
+    )
+    dq, dk, dv, dgate, own_grad = pl.pallas_call(
+        move_kernel,
+        out_shape=out_shape,
+        in_specs=[vmem] * 5,
+        out_specs=(hbm,) * 5,
+        scratch_shapes=[pltpu.SemaphoreType.DMA((5,))],
+        compiler_params=pltpu.CompilerParams(vmem_limit_bytes=4 * 2**20),
+        name="store_grads",
+    )(*grads)
+    return (dq, dk, dv, dgate, own_grad.T)
 
 
 def solution(mesh):

time: 92.1 us -> 83.3 us (0.904)
  local copies, waits for them, and re-layouts: 7.27 us -> 0 us
  matrix products: 1.41 us -> 0 us
  Pallas kernels: 81.1 us -> 82.5 us
  other arithmetic: 1.24 us -> 0 us
    unnamed x25 -> x0, local copies, waits for them, and re-layouts: 6.7 us -> none
    pallas_call x1 -> x2, Pallas kernels: 81.1 us -> 82.5 us  [the longest x1 81.3 us: local(): pl.pallas_call(kernel, out_shape=out_shape, in_specs=[hbm] * 10, out_spec...]
    dot_general x1 -> x0, matrix products: 1.41 us -> none  [local(): logits = jnp.dot(hidden_in, beta_weight, preferred_element_type=jnp.float32)]
where the time goes in v2:
time: 83.3 us; the launch traced here: 83.1 us
  Pallas kernels  82.5 us (99%)
    pallas_call x1, Pallas kernels, local(): pl.pallas_call(kernel, out_shape=out_shape, in_specs=[hbm] * 10, out_spec...  81.3 us

profile of v2, /device:TPU:0, one launch (start us, length us, event | category | flops | bytes accessed | tf_op | source)
XLA Modules:
  0.0 83.1 jit_solution(4893966608172557813)
XLA Ops:
  0.6 81.3 %delta_backward.1 = (bf16[128,2048]{1,0:T(8,128)(2,1)S(1)}, bf16[128,2048]{1,0:T(8,128)(2,1)S(1)}, bf16[128,2048]{1,0:T(8,128)(2,1)S(1)}, f32[16,128]{1,0:T(8,128)S(1)}, f32[16,72]{1,0:T(8,128)S(1)}) custom-call(s32[1,4]{1,0:T(1,128)} %length_in.1, f32[16]{0:T(128)} %reward_in.1, s32[16]{0:T(128)} %prompt_in.1, bf16[128,2048]{1,0:T(8,128)(2,1)} %q_in.1, ...), custom_call_target="tpu_custom_call" | custom-call | tf_op jit(solution)/shard_map/delta_backward/pallas_call | solution.py:517
  81.9 1.2 %store_grads.1 = (bf16[128,2048]{1,0:T(8,128)(2,1)}, bf16[128,2048]{1,0:T(8,128)(2,1)}, bf16[128,2048]{1,0:T(8,128)(2,1)}, f32[16,128]{1,0:T(8,128)}, f32[16,72]{1,0:T(8,128)}) custom-call(bf16[128,2048]{1,0:T(8,128)(2,1)S(1)} %get-tuple-element.15.refs_0_, bf16[128,2048]{1,0:T(8,128)(2,1)S(1)} %get-tuple-element.16.refs_1_, ...), custom_call_target="tpu_custom_call" | custom-call | tf_op jit(solution)/shard_map/store_grads/pallas_call | solution.py:564

commit v3 on v2

--- a/solution.py
+++ b/solution.py
@@ -10,6 +10,10 @@
 SMALL = 16
 MAP_LAG = 2
 GRAD_SLACK = 1
+DETOUR_LAG = 2
+MANY = (1, 3, 5)
+FEW = (3,)
+EXTRA = (4,)
 MESH = pl.DeviceIdType.MESH
 F32 = jnp.float32
 BF16 = jnp.bfloat16
@@ -97,11 +101,12 @@
     length_ref, reward_ref, prompt_ref,
     q_ref, k_ref, v_ref, o_ref, hidden_ref, proj_ref, gate_ref, cols_ref, rows_ref, load_sem,
     inv_ref, mix_ref, dkk_ref, dec_ref, maps_ref, give_ref,
-    fpair_ref, bpair_ref, fout_ref, bout_ref, fmate_ref, bmate_ref,
-    dlogit_ref, whole_ref, near_out, near_in, far_out, far_in,
+    detour_ref, fpair_ref, bpair_ref, fout_ref, bout_ref, fmate_ref, bmate_ref,
+    dlogit_ref,
     msend, mrecv, fsend, frecv, bsend, brecv, fgive, ftake, bgive, btake,
-    nsend, nrecv, wsend, wrecv,
+    dsend, drecv, *sums,
 ):
+    early, late = sums[:len(sums) // 2], sums[len(sums) // 2:]
     tokens = q_ref.shape[0]
     width = fout_ref.shape[-1]
     turns = fout_ref.shape[0]
@@ -204,8 +209,48 @@
             device_id={"ctx": to}, device_id_type=MESH,
         )
 
+    first_tier, last_tier = tier == 0, tier == tiers - 1
+    low, high = side == 0, side == 1
+    sends_one = (first_tier & low) | (last_tier & high)
+    takes_one = (first_tier & high) | (last_tier & low)
+
+    def among(i, some):
+        return functools.reduce(jnp.logical_or, [i == n for n in some])
+
+    lower_mid, upper_mid = tier == 1, tier == tiers - 2
+
+    def goes_down(i):
+        edge = lower_mid & ((low & among(i, MANY)) | (high & among(i, FEW)))
+        return (tiers >= 4) & (edge | (upper_mid & low & among(i, EXTRA)))
+
+    def goes_up(i):
+        edge = upper_mid & ((high & among(i, MANY)) | (low & among(i, FEW)))
+        return (tiers >= 4) & (edge | (lower_mid & high & among(i, EXTRA)))
+
+    def passes_up(i):
+        edge = first_tier & ((high & among(i, MANY)) | (low & among(i, FEW)))
+        return (tiers >= 4) & (edge | ((tier == tiers - 3) & high & among(i, EXTRA)))
+
+    def passes_down(i):
+        edge = last_tier & ((low & among(i, MANY)) | (high & among(i, FEW)))
+        return (tiers >= 4) & (edge | ((tier == 2) & low & among(i, EXTRA)))
+
     def map_copy(i):
         return copy(give_ref.at[i], maps_ref.at[i, side], msend.at[i], mrecv.at[i], mate)
+
+    def one_copy(i):
+        return copy(
+            give_ref.at[i, 1 + side], maps_ref.at[i, side, 1 + side], msend.at[i], mrecv.at[i],
+            mate,
+        )
+
+    def detour_copy(i):
+        via = mate + jnp.where(goes_down(i), -2, 2)
+        return copy(give_ref.at[i], detour_ref.at[i], msend.at[i], drecv.at[i], via)
+
+    def pass_copy(i):
+        to = seg + jnp.where(passes_up(i), 2, -2)
+        return copy(detour_ref.at[i], maps_ref.at[i, 1 - side], dsend.at[i], mrecv.at[i], to)
 
     def forward_copy(i):
         return copy(fout_ref.at[i], fpair_ref.at[i, 0], fsend.at[i], frecv.at[i], seg + 2)
@@ -283,46 +328,62 @@
             out[2] = t_mul(load(o_ref, h) * weight, carry)
 
     def forward_step(i):
-        @pl.when(tier == 0)
+        @pl.when(first_tier)
         def _():
             fpair_ref[i, 0] = jnp.zeros((width, width), F32)
-
-        @pl.when(tier > 0)
+            fpair_ref[i, 1] = maps_ref[i, 0, 1]
+
+        @pl.when(jnp.logical_not(first_tier))
         def _():
             forward_copy(i).wait_recv()
-
-        second = mul(fpair_ref[i, 0], maps_ref[i, 0, 0]) + maps_ref[i, 0, 1]
-        fpair_ref[i, 1] = second
-
-        @pl.when(tier < tiers - 1)
+            fpair_ref[i, 1] = mul(fpair_ref[i, 0], maps_ref[i, 0, 0]) + maps_ref[i, 0, 1]
+
+        @pl.when(jnp.logical_not(last_tier))
         def _():
             fout_ref[i] = mul(fpair_ref[i, 1], maps_ref[i, 1, 0]) + maps_ref[i, 1, 1]
             forward_copy(i).start()
 
-        state_copy(i).start()
+        @pl.when(jnp.logical_not(first_tier & high))
+        def _():
+            state_copy(i).start()
 
     def backward_step(i):
-        @pl.when(tier == tiers - 1)
+        @pl.when(last_tier)
         def _():
             bpair_ref[i, 1] = jnp.zeros((width, width), F32)
-
-        @pl.when(tier < tiers - 1)
+            bpair_ref[i, 0] = maps_ref[i, 1, 2]
+
+        @pl.when(jnp.logical_not(last_tier))
         def _():
             backward_copy(i).wait_recv()
-
-        first = mul_t(bpair_ref[i, 1], maps_ref[i, 1, 0]) + maps_ref[i, 1, 2]
-        bpair_ref[i, 0] = first
-
-        @pl.when(tier > 0)
+            bpair_ref[i, 0] = mul_t(bpair_ref[i, 1], maps_ref[i, 1, 0]) + maps_ref[i, 1, 2]
+
+        @pl.when(jnp.logical_not(first_tier))
         def _():
             bout_ref[i] = mul_t(bpair_ref[i, 0], maps_ref[i, 0, 0]) + maps_ref[i, 0, 2]
             backward_copy(i).start()
 
-        after_copy(i).start()
-
-    def gradient_part(turn):
-        state_copy(turn).wait_recv()
-        after_copy(turn).wait_recv()
+        @pl.when(jnp.logical_not(last_tier & low))
+        def _():
+            after_copy(i).start()
+
+    def gradient_first(turn):
+        @pl.when(first_tier & low)
+        def _():
+            fmate_ref[turn] = jnp.zeros((width, width), F32)
+
+        @pl.when(jnp.logical_not(first_tier & low))
+        def _():
+            state_copy(turn).wait_recv()
+
+        @pl.when(last_tier & high)
+        def _():
+            bmate_ref[turn] = jnp.zeros((width, width), F32)
+
+        @pl.when(jnp.logical_not(last_tier & high))
+        def _():
+            after_copy(turn).wait_recv()
+
         upper = jnp.where(rows < cols, 1.0, 0.0).astype(BF16)
         upper = stack(upper, upper)
         keep = []
@@ -346,13 +407,25 @@
         ]
         drs = [t_mul(inv_ref[turn, i], dus[i]) for i in both_heads]
         squares = [mul_t(stack(dos[i], drs[i]), us[i]) for i in both_heads]
+        lows = []
+        for i in both_heads:
+            beta = keep[i][0]
+            dlow = jnp.where(rows > cols, -squares[i][tokens:], 0.0)
+            lowpart = dlow * dkk_ref[turn, i]
+            dbeta = row_sum(drs[i] * rests[i]) + row_sum(lowpart)
+            dlogit_ref[heads[i]] = dbeta * beta * (1.0 - beta)
+            lows.append((dlow, lowpart))
+        return upper, keep, afters, heads, us, dos, drs, squares, lows
+
+    def gradient_rest(turn, values):
+        upper, keep, afters, heads, us, dos, drs, squares, lows = values
         for i in both_heads:
             beta, weight, head, tail, qs, ks, qh, kh, state, qstate, kstate = keep[i]
             h = heads[i]
-            u, do, dr, rest, after = us[i], dos[i], drs[i], rests[i], afters[i]
-            decay, dkk = dec_ref[turn, i], dkk_ref[turn, i]
+            u, do, dr, after = us[i], dos[i], drs[i], afters[i]
+            decay = dec_ref[turn, i]
+            dlow, lowpart = lows[i]
             dmix = squares[i][:tokens]
-            dlow = jnp.where(rows > cols, -squares[i][tokens:], 0.0)
             inward = mul(stack(head * do, (-beta * head) * dr), state)
             uafter = mul(u, after)
             da = dmix * decay
@@ -365,7 +438,6 @@
             dq_ref[:, lanes(h)] = (qs * (dqh - qh * row_sum(qh * dqh))).astype(BF16)
             dk_ref[:, lanes(h)] = (ks * (dkh - kh * row_sum(kh * dkh))).astype(BF16)
             dv_ref[:, lanes(h)] = (beta * dr).astype(BF16)
-            lowpart = dlow * dkk
             spread = dmix * mix_ref[turn, i] + beta * lowpart
             across = lax.dot_general(
                 left(spread), upper, (((1,), (0,)), ((), ())), preferred_element_type=F32
@@ -377,8 +449,6 @@
             dgate_ref[pl.ds(h, 1), :] = jnp.sum(
                 jnp.where(rows >= cols, across + headgrad, tailgrad), axis=0, keepdims=True
             )
-            dbeta = row_sum(dr * rest) + row_sum(lowpart)
-            dlogit_ref[h] = dbeta * beta * (1.0 - beta)
 
     def within(i):
         return (i >= 0) & (i < turns)
@@ -389,7 +459,26 @@
         @pl.when(t < turns)
         def _():
             local_part(t)
-            map_copy(t).start()
+            detour = goes_down(t) | goes_up(t)
+
+            @pl.when(sends_one)
+            def _():
+                one_copy(t).start()
+
+            @pl.when(detour)
+            def _():
+                detour_copy(t).start()
+
+            @pl.when(jnp.logical_not(sends_one | detour))
+            def _():
+                map_copy(t).start()
+
+        d = t - DETOUR_LAG
+
+        @pl.when(within(d) & (passes_up(d) | passes_down(d)))
+        def _():
+            detour_copy(d).wait_recv()
+            pass_copy(d).start()
 
         f = t - MAP_LAG - tier
         b = t - MAP_LAG - (tiers - 1 - tier)
@@ -397,7 +486,13 @@
 
         @pl.when(within(m))
         def _():
-            map_copy(m).wait_recv()
+            @pl.when(takes_one)
+            def _():
+                one_copy(m).wait_recv()
+
+            @pl.when(jnp.logical_not(takes_one))
+            def _():
+                map_copy(m).wait_recv()
 
         @pl.when(within(f))
         def _():
@@ -409,75 +504,126 @@
 
         @pl.when(within(t - grad_lag))
         def _():
-            gradient_part(t - grad_lag)
+            g = t - grad_lag
+
+            @pl.when(g == cut)
+            def _():
+                early_begin()
+
+            values = gradient_first(g)
+
+            @pl.when(g == turns - 1)
+            def _():
+                late_begin()
+
+            gradient_rest(g, values)
+
+            @pl.when(g == cut)
+            def _():
+                early_middle()
 
         return unused
 
+
+    def drain(i, unused):
+        @pl.when(sends_one)
+        def _():
+            one_copy(i).wait_send()
+
+        @pl.when(jnp.logical_not(sends_one))
+        def _():
+            map_copy(i).wait_send()
+
+        @pl.when(passes_up(i) | passes_down(i))
+        def _():
+            pass_copy(i).wait_send()
+
+        @pl.when(jnp.logical_not(first_tier & high))
+        def _():
+            state_copy(i).wait_send()
+
+        @pl.when(jnp.logical_not(last_tier & low))
+        def _():
+            after_copy(i).wait_send()
+
+        @pl.when(jnp.logical_not(last_tier))
+        def _():
+            forward_copy(i).wait_send()
+
+        @pl.when(jnp.logical_not(first_tier))
+        def _():
+            backward_copy(i).wait_send()
+
+        return unused
+
+    hidden = hidden_ref[...]
+    hidden = stack(hidden, hidden)
+
+    def reduction(some, whole_ref, near_out, near_in, far_out, far_in, nsend, nrecv, wsend, wrecv):
+        owned = weight_ref.shape[1]
+        breadth = near_out.shape[-1]
+        model = hidden.shape[1]
+
+        def near_copy(by):
+            to = lax.rem(part + by, parts)
+            return pltpu.make_async_remote_copy(
+                src_ref=near_out.at[to], dst_ref=near_in.at[by - 1],
+                send_sem=nsend.at[by - 1], recv_sem=nrecv.at[by - 1],
+                device_id={"dp": to}, device_id_type=MESH,
+            )
+
+        def far_copy(by):
+            to = lax.rem(seg + by, count)
+            return copy(far_out.at[to], far_in.at[by - 1], wsend.at[by - 1], wrecv.at[by - 1], to)
+
+        def begin():
+            logit_grad = jnp.concatenate([dlogit_ref[h] for h in some], axis=1)
+            whole_ref[:, model:] = jnp.zeros_like(whole_ref[:, model:])
+            whole_ref[:, :model] = lax.dot_general(
+                left_t(logit_grad), hidden, (((0,), (0,)), ((), ())), preferred_element_type=F32
+            )
+            for p in range(parts):
+                for c in range(count):
+                    at = (p * count + c) * owned
+                    near_out[p, c] = whole_ref[:, at:at + breadth]
+            for by in range(1, parts):
+                near_copy(by).start()
+
+        def middle():
+            total = near_out[part]
+            for by in range(1, parts):
+                near_copy(by).wait_recv()
+                total = total + near_in[by - 1]
+            far_out[...] = total
+            for by in range(1, count):
+                far_copy(by).start()
+
+        def end():
+            total = far_out[seg]
+            for by in range(1, count):
+                far_copy(by).wait_recv()
+                total = total + far_in[by - 1]
+            for by in range(1, parts):
+                near_copy(by).wait_send()
+            for by in range(1, count):
+                far_copy(by).wait_send()
+            return total[:, :owned]
+
+        return begin, middle, end
+
+    def heads_of(some):
+        return [n for n in some] + [turns + n for n in some]
+
+    cut = turns - 2
+    early_begin, early_middle, early_end = reduction(heads_of(range(cut)), *early)
+    late_begin, late_middle, late_end = reduction(heads_of(range(cut, turns)), *late)
+
     lax.fori_loop(0, turns + grad_lag, step, 0)
-
-    def drain(i, unused):
-        map_copy(i).wait_send()
-        state_copy(i).wait_send()
-        after_copy(i).wait_send()
-
-        @pl.when(tier < tiers - 1)
-        def _():
-            forward_copy(i).wait_send()
-
-        @pl.when(tier > 0)
-        def _():
-            backward_copy(i).wait_send()
-
-        return unused
-
-    logit_grad = jnp.concatenate([dlogit_ref[h] for h in range(2 * turns)], axis=1)
-    hidden = hidden_ref[...]
-    whole_ref[...] = lax.dot_general(
-        left_t(logit_grad), stack(hidden, hidden), (((0,), (0,)), ((), ())),
-        preferred_element_type=F32,
-    )
-    owned = near_out.shape[-1]
-    for p in range(parts):
-        for c in range(count):
-            at = (p * count + c) * owned
-            near_out[p, c] = whole_ref[:, at:at + owned]
-
-    def near_copy(by):
-        to = lax.rem(part + by, parts)
-        return pltpu.make_async_remote_copy(
-            src_ref=near_out.at[to], dst_ref=near_in.at[by - 1],
-            send_sem=nsend.at[by - 1], recv_sem=nrecv.at[by - 1],
-            device_id={"dp": to}, device_id_type=MESH,
-        )
-
-    def far_copy(by):
-        to = lax.rem(seg + by, count)
-        return pltpu.make_async_remote_copy(
-            src_ref=far_out.at[to], dst_ref=far_in.at[by - 1],
-            send_sem=wsend.at[by - 1], recv_sem=wrecv.at[by - 1],
-            device_id={"ctx": to}, device_id_type=MESH,
-        )
-
-    for by in range(1, parts):
-        near_copy(by).start()
-    total = near_out[part]
-    for by in range(1, parts):
-        near_copy(by).wait_recv()
-        total = total + near_in[by - 1]
-    far_out[...] = total
-    for by in range(1, count):
-        far_copy(by).start()
-    total = far_out[seg]
-    for by in range(1, count):
-        far_copy(by).wait_recv()
-        total = total + far_in[by - 1]
-    weight_ref[...] = total
-    for by in range(1, parts):
-        near_copy(by).wait_send()
-    for by in range(1, count):
-        far_copy(by).wait_send()
-
+    late_middle()
     lax.fori_loop(0, turns, drain, 0)
+    most = early_end()
+    few = late_end()
+    weight_ref[...] = stack(most[:cut], few[:2], most[cut:], few[2:])
 
 
 def move_kernel(*refs):
@@ -507,6 +653,7 @@
     model = hidden_in.shape[1]
     dp_count = lax.axis_size("dp")
     owned = model // (dp_count * ctx_count)
+    breadth = -(-owned // 128) * 128
     out_shape = (
         jax.ShapeDtypeStruct(queries.shape, BF16),
         jax.ShapeDtypeStruct(queries.shape, BF16),
@@ -514,6 +661,20 @@
         jax.ShapeDtypeStruct((heads, tokens), F32),
         jax.ShapeDtypeStruct((heads, owned), F32),
     )
+
+    def reduction_scratch(some):
+        return [
+            pltpu.VMEM((some, model + breadth), F32),
+            pltpu.VMEM((dp_count, ctx_count, some, breadth), F32),
+            pltpu.VMEM((dp_count - 1 or 1, ctx_count, some, breadth), F32),
+            pltpu.VMEM((ctx_count, some, breadth), F32),
+            pltpu.VMEM((ctx_count - 1, some, breadth), F32),
+            pltpu.SemaphoreType.DMA((dp_count,)),
+            pltpu.SemaphoreType.DMA((dp_count,)),
+            pltpu.SemaphoreType.DMA((ctx_count,)),
+            pltpu.SemaphoreType.DMA((ctx_count,)),
+        ]
+
     grads = pl.pallas_call(
         kernel,
         out_shape=out_shape,
@@ -537,20 +698,16 @@
         + [
             pltpu.VMEM((turns, 2, 3, width, width), F32),
             pltpu.VMEM((turns, 3, width, width), F32),
+            pltpu.VMEM((turns, 3, width, width), F32),
         ]
         + [pltpu.VMEM(pairs, F32)] * 2
         + [pltpu.VMEM(states, F32)] * 4
         + [
             pltpu.VMEM((heads, tokens, 1), F32),
-            pltpu.VMEM((heads, model), F32),
-            pltpu.VMEM((dp_count, ctx_count, heads, owned), F32),
-            pltpu.VMEM((dp_count - 1 or 1, ctx_count, heads, owned), F32),
-            pltpu.VMEM((ctx_count, heads, owned), F32),
-            pltpu.VMEM((ctx_count - 1, heads, owned), F32),
         ]
-        + [pltpu.SemaphoreType.DMA((turns,))] * 10
-        + [pltpu.SemaphoreType.DMA((dp_count,))] * 2
-        + [pltpu.SemaphoreType.DMA((ctx_count,))] * 2,
+        + [pltpu.SemaphoreType.DMA((turns,))] * 12
+        + reduction_scratch(heads - 4)
+        + reduction_scratch(4),
         compiler_params=pltpu.CompilerParams(
             collective_id=0, has_side_effects=True, vmem_limit_bytes=48 * 2**20
         ),

time: 83.3 us -> 79.9 us (0.959)
  Pallas kernels: 82.5 us -> 79 us
    pallas_call x1, Pallas kernels: 81.3 us -> 77.9 us  [local(): pl.pallas_call(kernel, out_shape=out_shape, in_specs=[hbm] * 10, out_spec...]
where the time goes in v3:
time: 79.9 us; the launch traced here: 79.7 us
  Pallas kernels  79 us (99%)
    pallas_call x1, Pallas kernels, local(): pl.pallas_call(kernel, out_shape=out_shape, in_specs=[hbm] * 10, out_spec...  77.9 us

profile of v3, /device:TPU:0, one launch (start us, length us, event | category | flops | bytes accessed | tf_op | source)
XLA Modules:
  0.0 79.7 jit_solution(17567226139921910202)
XLA Ops:
  0.6 77.9 %delta_backward.1 = (bf16[128,2048]{1,0:T(8,128)(2,1)S(1)}, bf16[128,2048]{1,0:T(8,128)(2,1)S(1)}, bf16[128,2048]{1,0:T(8,128)(2,1)S(1)}, f32[16,128]{1,0:T(8,128)S(1)}, f32[16,72]{1,0:T(8,128)S(1)}) custom-call(s32[1,4]{1,0:T(1,128)} %length_in.1, f32[16]{0:T(128)} %reward_in.1, s32[16]{0:T(128)} %prompt_in.1, bf16[128,2048]{1,0:T(8,128)(2,1)} %q_in.1, ...), custom_call_target="tpu_custom_call" | custom-call | tf_op jit(solution)/shard_map/delta_backward/pallas_call | solution.py:678
  78.5 1.2 %store_grads.1 = (bf16[128,2048]{1,0:T(8,128)(2,1)}, bf16[128,2048]{1,0:T(8,128)(2,1)}, bf16[128,2048]{1,0:T(8,128)(2,1)}, f32[16,128]{1,0:T(8,128)}, f32[16,72]{1,0:T(8,128)}) custom-call(bf16[128,2048]{1,0:T(8,128)(2,1)S(1)} %get-tuple-element.15.refs_0_, bf16[128,2048]{1,0:T(8,128)(2,1)S(1)} %get-tuple-element.16.refs_1_, ...), custom_call_target="tpu_custom_call" | custom-call | tf_op jit(solution)/shard_map/store_grads/pallas_call | solution.py:721

commit v4 on v3

--- a/solution.py
+++ b/solution.py
@@ -11,9 +11,9 @@
 MAP_LAG = 2
 GRAD_SLACK = 1
 DETOUR_LAG = 2
-MANY = (1, 3, 5)
-FEW = (3,)
-EXTRA = (4,)
+MANY = (0, 2, 4)
+FEW = (2,)
+EXTRA = (3,)
 MESH = pl.DeviceIdType.MESH
 F32 = jnp.float32
 BF16 = jnp.bfloat16
@@ -99,7 +99,7 @@
     q_in, k_in, v_in, o_in, hidden_in, proj_in, gate_in,
     dq_ref, dk_ref, dv_ref, dgate_ref, weight_ref,
     length_ref, reward_ref, prompt_ref,
-    q_ref, k_ref, v_ref, o_ref, hidden_ref, proj_ref, gate_ref, cols_ref, rows_ref, load_sem,
+    q_ref, k_ref, v_ref, o_ref, hidden_ref, proj_ref, gate_ref, cols_ref, rows_ref, table_ref, wide_ref, load_sem,
     inv_ref, mix_ref, dkk_ref, dec_ref, maps_ref, give_ref,
     detour_ref, fpair_ref, bpair_ref, fout_ref, bout_ref, fmate_ref, bmate_ref,
     dlogit_ref,
@@ -115,6 +115,8 @@
     tiers = count // 2
     tier = seg // 2
     side = lax.rem(seg, 2)
+    owned = weight_ref.shape[1]
+    breadth = wide_ref.shape[1] // (lax.axis_size("dp") * count)
     mate = seg + 1 - 2 * side
 
     loads = [
@@ -195,10 +197,19 @@
         hidden_ref[...], proj_ref[...], (((1,), (1,)), ((), ())), preferred_element_type=F32
     )
     betas = jax.nn.sigmoid(logits)
-    for h in range(heads_all):
-        cols_ref[h] = jnp.concatenate(
-            [betas[:, h:h + 1], gamma_cols[:, h:h + 1], number_col, weight_col], axis=1
-        )
+    turn_count = heads_all // 2
+    table_ref[0] = betas
+    table_ref[1] = gamma_cols
+    table_ref[2, :, :2] = jnp.concatenate([number_col, weight_col], axis=1)
+
+    def write_columns(some):
+        shared = table_ref[2, :, :2]
+        for h in some:
+            cols_ref[h] = jnp.concatenate(
+                [table_ref[0, :, h:h + 1], table_ref[1, :, h:h + 1], shared], axis=1
+            )
+
+    write_columns((0, turn_count))
     for load_copy in loads[6:]:
         load_copy.wait()
     pl.semaphore_wait(barrier, count + parts - 2)
@@ -473,6 +484,18 @@
             def _():
                 map_copy(t).start()
 
+        @pl.when(t == 0)
+        def _():
+            write_columns([h for h in range(heads_all) if h not in (0, turn_count)])
+
+        @pl.when(t == 1)
+        def _():
+            wide_ref[...] = jnp.zeros_like(wide_ref)
+            for n in range(parts * count):
+                wide_ref[:, n * breadth:n * breadth + owned] = (
+                    hidden_ref[:, n * owned:(n + 1) * owned]
+                )
+
         d = t - DETOUR_LAG
 
         @pl.when(within(d) & (passes_up(d) | passes_down(d)))
@@ -556,14 +579,7 @@
 
         return unused
 
-    hidden = hidden_ref[...]
-    hidden = stack(hidden, hidden)
-
-    def reduction(some, whole_ref, near_out, near_in, far_out, far_in, nsend, nrecv, wsend, wrecv):
-        owned = weight_ref.shape[1]
-        breadth = near_out.shape[-1]
-        model = hidden.shape[1]
-
+    def reduction(some, near_out, near_in, far_out, far_in, nsend, nrecv, wsend, wrecv):
         def near_copy(by):
             to = lax.rem(part + by, parts)
             return pltpu.make_async_remote_copy(
@@ -578,14 +594,15 @@
 
         def begin():
             logit_grad = jnp.concatenate([dlogit_ref[h] for h in some], axis=1)
-            whole_ref[:, model:] = jnp.zeros_like(whole_ref[:, model:])
-            whole_ref[:, :model] = lax.dot_general(
-                left_t(logit_grad), hidden, (((0,), (0,)), ((), ())), preferred_element_type=F32
+            wide = wide_ref[...]
+            sums = lax.dot_general(
+                left_t(logit_grad), stack(wide, wide), (((0,), (0,)), ((), ())),
+                preferred_element_type=F32,
             )
             for p in range(parts):
                 for c in range(count):
-                    at = (p * count + c) * owned
-                    near_out[p, c] = whole_ref[:, at:at + breadth]
+                    at = (p * count + c) * breadth
+                    near_out[p, c] = sums[:, at:at + breadth]
             for by in range(1, parts):
                 near_copy(by).start()
 
@@ -664,7 +681,6 @@
 
     def reduction_scratch(some):
         return [
-            pltpu.VMEM((some, model + breadth), F32),
             pltpu.VMEM((dp_count, ctx_count, some, breadth), F32),
             pltpu.VMEM((dp_count - 1 or 1, ctx_count, some, breadth), F32),
             pltpu.VMEM((ctx_count, some, breadth), F32),
@@ -692,6 +708,8 @@
             pltpu.VMEM(log_gate.shape, F32),
             pltpu.VMEM((heads, tokens, 4), F32),
             pltpu.VMEM((heads, 2, tokens), F32),
+            pltpu.VMEM((3, tokens, heads), F32),
+            pltpu.VMEM((tokens, dp_count * ctx_count * breadth), BF16),
             pltpu.SemaphoreType.DMA((10,)),
         ]
         + [pltpu.VMEM(square, F32)] * 4

time: 79.9 us -> 79.7 us (level)
  no operation moved by 1% of the time
where the time goes in v4:
time: 79.7 us; the launch traced here: 79.6 us
  Pallas kernels  78.9 us (99%)
    pallas_call x1, Pallas kernels, local(): pl.pallas_call(kernel, out_shape=out_shape, in_specs=[hbm] * 10, out_spec...  77.7 us

profile of v4, /device:TPU:0, one launch (start us, length us, event | category | flops | bytes accessed | tf_op | source)
XLA Modules:
  0.0 79.6 jit_solution(1722535416829945071)
XLA Ops:
  0.6 77.7 %delta_backward.1 = (bf16[128,2048]{1,0:T(8,128)(2,1)S(1)}, bf16[128,2048]{1,0:T(8,128)(2,1)S(1)}, bf16[128,2048]{1,0:T(8,128)(2,1)S(1)}, f32[16,128]{1,0:T(8,128)S(1)}, f32[16,72]{1,0:T(8,128)S(1)}) custom-call(s32[1,4]{1,0:T(1,128)} %length_in.1, f32[16]{0:T(128)} %reward_in.1, s32[16]{0:T(128)} %prompt_in.1, bf16[128,2048]{1,0:T(8,128)(2,1)} %q_in.1, ...), custom_call_target="tpu_custom_call" | custom-call | tf_op jit(solution)/shard_map/delta_backward/pallas_call | solution.py:694
  78.4 1.2 %store_grads.1 = (bf16[128,2048]{1,0:T(8,128)(2,1)}, bf16[128,2048]{1,0:T(8,128)(2,1)}, bf16[128,2048]{1,0:T(8,128)(2,1)}, f32[16,128]{1,0:T(8,128)}, f32[16,72]{1,0:T(8,128)}) custom-call(bf16[128,2048]{1,0:T(8,128)(2,1)S(1)} %get-tuple-element.15.refs_0_, bf16[128,2048]{1,0:T(8,128)(2,1)S(1)} %get-tuple-element.16.refs_1_, ...), custom_call_target="tpu_custom_call" | custom-call | tf_op jit(solution)/shard_map/store_grads/pallas_call | solution.py:739
